TPU v7x, 32 devices: a whole 2x2x4 slice. The times are simulated.
32 devices in a mesh: groups: 2 (over y), dp: 16 (over z, x, core).
Axes of the slice: x: 2, y: 2, z: 4, core: 2. Of those that a mesh axis runs over, the one named last changes fastest.
Arguments:
- particles: bfloat16 [2048, 128, 128], P(('groups', 'dp')), parts along dimension 0, may hold values from -20 to 20
- refs: bfloat16 [128, 256, 128], P('dp', 'groups'), parts along dimension 1, may hold values from -0.5 to 0.5
- ctf_group: int32 [2048], P(('groups', 'dp')), parts along dimension 0, may hold values from 0 to 31, as said below
- defocus: float32 [64], P('groups'), parts along dimension 0, may hold values from 0.5 to 2
- class_prior: float32 [256], P('groups'), parts along dimension 0, may hold values from 0.25 to 4
- cycle_weight: float32 [64], replicated, may hold values from 0.5 to 2
Outputs:
- new_refs: float32 [128, 256, 128], P('dp', 'groups'), parts along dimension 1
- log_evidence: float32 [2048], P(('groups', 'dp')), parts along dimension 0
There are 2 independent parts, one for each index of `groups`. A program takes and returns all parts, laid end to end along the dimension named above; an argument that names none is the same for every part. Nothing has to cross between parts.
Inputs may be any that keep to these rules, and one draw needn't show every extreme that they name: `ctf_group`: CTF groups follow the particle order: particle n belongs to group n * 32 // 1024 or the next one, capped at 31.
All inputs are finite; a program needn't handle non-finite values.
Results may differ from a plain program's by a relative error of at most 0.0045.
Values may be sent and summed in bfloat16 or wider, within the bound.
A program may use at most 64 MiB of HBM per device.

v0:
```python
import math
import jax
import jax.numpy as jnp
from jax import lax
from jax.sharding import PartitionSpec as P

M = 128
R = 64
ROT = 36
G = 32


def ctf_table(defocus):
    radius = (jnp.arange(R, dtype=jnp.float32) + 1.0) / R
    phase = 20.0 * defocus[:, None] * radius[None, :] ** 2
    return -(0.995 * jnp.sin(phase) + 0.1 * jnp.cos(phase))


def angle_tables():
    harmonic = jnp.arange(M, dtype=jnp.float32)[:, None]
    turning = jnp.arange(ROT, dtype=jnp.float32)[None, :]
    theta = 2.0 * math.pi * harmonic * turning / ROT
    return (jnp.cos(theta), jnp.sin(theta))


def shards(particles, refs, ctf_group, defocus, class_prior, cycle_weight):
    highest = lax.Precision.HIGHEST
    ctf = ctf_table(defocus)
    cos_table, sin_table = angle_tables()
    onehot = (ctf_group[:, None] == jnp.arange(G, dtype=jnp.int32)[None, :]).astype(jnp.float32)
    gain_table = jnp.concatenate([cycle_weight[None, :] * ctf, cycle_weight[None, :] * ctf], axis=1)
    gain = jnp.dot(onehot, gain_table, precision=highest)
    weighted = (particles.astype(jnp.float32) * gain[:, None, :]).astype(jnp.bfloat16)
    turned = jnp.concatenate([weighted[:, :, R:], -weighted[:, :, :R]], axis=2)
    all_refs = lax.all_gather(refs, "dp", axis=0, tiled=True)
    part_weighted = weighted
    part_turned = turned
    part_cos = cos_table
    part_sin = sin_table
    cross_real = jnp.einsum(
        "nmq,mkq->mnk", part_weighted, all_refs, preferred_element_type=jnp.float32
    )
    cross_imag = jnp.einsum(
        "nmq,mkq->mnk", part_turned, all_refs, preferred_element_type=jnp.float32
    )
    corr = jnp.einsum("mnk,mj->jnk", cross_real, part_cos, precision=highest)
    corr = corr - jnp.einsum("mnk,mj->jnk", cross_imag, part_sin, precision=highest)
    wide_refs = all_refs.astype(jnp.float32)
    energy = jnp.sum(wide_refs[:, :, :R] ** 2 + wide_refs[:, :, R:] ** 2, axis=0)
    corr, energy = (corr, energy)
    quadratic = jnp.dot(cycle_weight[None, :] * ctf * ctf, energy.T, precision=highest)
    norm_term = jnp.dot(onehot, quadratic, precision=highest)
    scores = corr - 0.5 * norm_term[None, :, :] + jnp.log(class_prior)[None, None, :]
    top = jnp.max(scores, axis=(0, 2), keepdims=True)
    expo = jnp.exp(scores - top)
    total = jnp.sum(expo, axis=(0, 2), keepdims=True)
    posterior = expo / total
    log_evidence = top[0, :, 0] + jnp.log(total[0, :, 0])
    local_mass = jnp.dot(onehot.T, jnp.sum(posterior, axis=0), precision=highest)
    mass = lax.psum(local_mass, "dp")
    part_cos = cos_table
    part_sin = sin_table
    post_real = jnp.einsum("jnk,mj->mnk", posterior, part_cos, precision=highest).astype(
        jnp.bfloat16
    )
    post_imag = jnp.einsum("jnk,mj->mnk", posterior, part_sin, precision=highest).astype(
        jnp.bfloat16
    )
    part_weighted = weighted
    part_turned = turned
    term = jnp.einsum("mnk,nmq->mkq", post_real, part_weighted, preferred_element_type=jnp.float32)
    numer = lax.psum_scatter(
        term
        - jnp.einsum("mnk,nmq->mkq", post_imag, part_turned, preferred_element_type=jnp.float32),
        "dp",
        scatter_dimension=0,
        tiled=True,
    )
    denom = 1.0 + jnp.dot(mass.T, cycle_weight[None, :] * ctf * ctf, precision=highest)
    denom_wide = jnp.concatenate([denom, denom], axis=1)
    new_refs = numer / denom_wide[None, :, :]
    return (new_refs, log_evidence)


def solution(mesh):
    in_specs = (
        P(("groups", "dp"), None, None),
        P("dp", "groups", None),
        P(("groups", "dp")),
        P("groups"),
        P("groups"),
        P(),
    )
    out_specs = (P("dp", "groups", None), P(("groups", "dp")))
    return jax.shard_map(shards, mesh=mesh, in_specs=in_specs, out_specs=out_specs, check_vma=False)
```

profile of v0, /device:TPU:0, one launch (start us, length us, event | category | flops | bytes accessed | tf_op | source)
XLA Modules:
  0.0 214.6 jit_solution(5967293046546979658)
XLA Ops:
  7.2 0.7 all-gather.2.cloned.1.call-update
  7.9 0.7 log.6
  8.6 0.7 broadcast_multiply_fusion
  9.3 0.8 fusion.38
  10.1 0.9 fusion.20
  11.0 2.9 %multiply_convert_fusion = bf16[64,128,128]{2,0,1:T(8,128)(2,1)S(1)} fusion(bf16[64,128,128]{2,1,0:T(8,128)(2,1)} %param.6, f32[64,128]{1,0:T(8,128)S(1)} %fusion.20), kind=kLoop, calls=%fused_computation.10 | loop fusion | flops 3145728 | bytes 4227072 | tf_op jit(solution)/shard_map/convert_element_type | solution.py:33
  13.9 2.7 %fusion.70 = (bf16[64,128,64]{2,0,1:T(8,128)(2,1)}, bf16[64,128,64]{2,0,1:T(8,128)(2,1)}) fusion(bf16[64,128,128]{2,0,1:T(8,128)(2,1)S(1)} %multiply_convert_fusion), kind=kLoop, calls=%fused_computation.77 | loop fusion | flops 524288 | bytes 4194304 | tf_op jit(solution)/shard_map/slice | solution.py:34
  16.6 46.6 %all-gather.2.cloned.1.call-done = bf16[128,128,128]{2,1,0:T(8,128)(2,1)} async-done(((bf16[8,128,128]{2,1,0:T(8,128)(2,1)}), bf16[128,128,128]{2,1,0:T(8,128)(2,1)}) %all-gather.2.cloned.1.call-update) | async-done | bytes 4194320 | tf_op jit(solution)/shard_map/all_gather | solution.py:35
  63.3 3.2 %convert_element_type.18 = f32[128,128,128]{2,1,0:T(8,128)S(1)} convert(bf16[128,128,128]{2,1,0:T(8,128)(2,1)} %all-gather.2.cloned.1.call-done) | non-fusion elementwise | flops 2097152 | bytes 12582912 | tf_op jit(solution)/shard_map/convert_element_type | solution.py:48
  66.6 2.5 %fusion.1 = f32[128,64]{1,0:T(8,128)S(1)} fusion(f32[128,128,128]{2,1,0:T(8,128)S(1)} %convert_element_type.18), kind=kLoop, calls=%fused_computation.2 | loop fusion | flops 4186112 | bytes 8421376 | tf_op jit(solution)/shard_map/reduce_sum | solution.py:49
  70.0 3.0 %fusion.18 = f32[128,64,128]{2,1,0:T(8,128)S(1)} fusion(bf16[128,128,128]{2,1,0:T(8,128)(2,1)S(1)} %copy-done, bf16[64,128,64]{2,0,1:T(8,128)(2,1)S(1)} %copy-done.2, bf16[64,128,64]{2,0,1:T(8,128)(2,1)S(1)} %copy-done.1), kind=kOutput, calls=%fused_computation.23 | convolution fusion | flops 272629760 | bytes 10485760 | tf_op jit(solution)/shard_map/nmq,mkq->mnk/dot_general | solution.py:43
  73.0 4.7 %fusion.2 = f32[36,64,128]{2,0,1:T(8,128)S(1)} fusion(f32[128,64,128]{2,1,0:T(8,128)S(1)} %fusion.18, f32[128]{0:T(128)S(1)} %iota_multiply_fusion), kind=kOutput, calls=%fused_computation.6 | convolution fusion | flops 452994048 | bytes 5374464 | tf_op jit(solution)/shard_map/mnk,mj->jnk/dot_general | solution.py:47
  77.7 3.0 %fusion.72 = f32[128,64,128]{2,1,0:T(8,128)S(1)} fusion(bf16[64,128,128]{2,0,1:T(8,128)(2,1)S(1)} %multiply_convert_fusion, bf16[128,128,128]{2,1,0:T(8,128)(2,1)S(1)} %copy-done), kind=kOutput, calls=%fused_computation.79 | convolution fusion | flops 268435456 | bytes 10485760 | tf_op jit(solution)/shard_map/nmq,mkq->mnk/dot_general | solution.py:40
  80.6 5.3 %fusion.71 = (f32[64]{0:T(128)S(1)}, f32[36,64,128]{2,0,1:T(8,128)S(1)}) fusion(f32[128]{0:T(128)S(1)} %log.6, f32[64,128]{1,0:T(8,128)S(1)} %convolution_multiply_fusion, f32[36,64,128]{2,0,1:T(8,128)S(1)} %fusion.2, f32[128,64,128]{2,1,0:T(8,128)S(1)} %fusion.72, f32[128]{0:T(128)S(1)} %iota_multiply_fusion), kind=kOutput, calls=%fused_computation.78 | convolution fusion | flops 454173632 | bytes 6587648 | tf_op jit(solution)/shard_map/mnk,mj->jnk/dot_general | solution.py:46
  85.9 1.0 fusion.17
  86.9 3.9 %fusion.24 = bf16[128,64,128]{2,0,1:T(8,128)(2,1)S(1)} fusion(f32[128]{0:T(128)S(1)} %iota_multiply_fusion, f32[36,64,128]{2,0,1:T(8,128)S(1)} %get-tuple-element.5, f32[64]{0:T(128)S(1)} %fusion.17, f32[64]{0:T(128)S(1)} %get-tuple-element.4), kind=kOutput, calls=%fused_computation.34 | convolution fusion | flops 453583872 | bytes 3277824 | tf_op jit(solution)/shard_map/jnk,mj->mnk/dot_general | solution.py:63
  90.8 3.9 %fusion.21 = bf16[128,64,128]{2,0,1:T(8,128)(2,1)S(1)} fusion(f32[128]{0:T(128)S(1)} %iota_multiply_fusion, f32[36,64,128]{2,0,1:T(8,128)S(1)} %get-tuple-element.5, f32[64]{0:T(128)S(1)} %fusion.17, f32[64]{0:T(128)S(1)} %get-tuple-element.4), kind=kOutput, calls=%fused_computation.31 | convolution fusion | flops 453583872 | bytes 3277824 | tf_op jit(solution)/shard_map/jnk,mj->mnk/dot_general | solution.py:66
  94.7 2.0 fusion.6
  96.7 6.8 %convolution_subtract_fusion = f32[128,128,128]{2,1,0:T(8,128)} fusion(f32[128,128,128]{2,1,0:T(8,128)S(1)} %fusion.6, bf16[128,64,128]{2,0,1:T(8,128)(2,1)S(1)} %fusion.21, bf16[64,128,64]{2,0,1:T(8,128)(2,1)S(1)} %copy-done.2, bf16[64,128,64]{2,0,1:T(8,128)(2,1)S(1)} %copy-done.1), kind=kOutput, calls=%fused_computation.11 | convolution fusion | flops 274726912 | bytes 20971520 | tf_op jit(solution)/shard_map/mnk,nmq->mkq/dot_general | solution.py:74
  104.1 61.6 %psum.7 = f32[32,128]{1,0:T(8,128)S(1)} all-reduce(f32[32,128]{1,0:T(8,128)S(1)} %fusion.19), channel_id=1, replica_groups=mesh['groups'=2,'dp'=16] {'dp'}, use_global_device_ids=true, to_apply=%region_5.0 | all-reduce | flops 4096 | bytes 32768 | tf_op jit(solution)/shard_map/psum | solution.py:60
  165.7 0.4 convolution_add_fusion
  166.2 0.5 log_add_fusion
  166.8 39.1 %reduce-scatter.2.cloned.1.call-done = f32[8,128,128]{2,1,0:T(8,128)} async-done(((f32[128,128,128]{2,1,0:T(8,128)}), f32[8,128,128]{2,1,0:T(8,128)}) %reduce-scatter.2.cloned.1.call-update) | async-done | bytes 524304 | tf_op jit(solution)/shard_map/reduce_scatter | solution.py:72
  205.9 1.9 broadcast_divide_fusion
  (21 shorter events, 1.7 us)
Async XLA Ops:
  7.2 56.1 %all-gather.2.cloned.1.call-start = ((), (), s32[]{:S(2)}) async-start(), calls=%async_computation.1 | async-start | bytes 4456448 | tf_op jit(solution)/shard_map/all_gather | solution.py:35
  7.9 198.0 %reduce-scatter.2.cloned.1.call-start = ((), (), s32[]{:S(2)}) async-start(), calls=%async_computation.2 | async-start | bytes 8912896 | tf_op jit(solution)/shard_map/reduce_scatter | solution.py:72
  66.5 2.6 %copy-start.3 = (f32[64]{0:T(128)S(1)}, f32[64]{0:T(128)}, u32[]{:S(2)}) copy-start(f32[64]{0:T(128)} %param.11) | copy-start | bytes 772
  66.5 2.9 %copy-start.4 = (s32[64]{0:T(128)S(1)}, s32[64]{0:T(128)}, u32[]{:S(2)}) copy-start(s32[64]{0:T(128)} %param.8) | copy-start | bytes 772
  66.5 3.1 %copy-start = (bf16[128,128,128]{2,1,0:T(8,128)(2,1)S(1)}, bf16[128,128,128]{2,1,0:T(8,128)(2,1)}, u32[]{:S(2)}) copy-start(bf16[128,128,128]{2,1,0:T(8,128)(2,1)} %all-gather.2.cloned.1.call-done) | copy-start | bytes 12582916
  66.5 3.1 %copy-start.1 = (bf16[64,128,64]{2,0,1:T(8,128)(2,1)S(1)}, bf16[64,128,64]{2,0,1:T(8,128)(2,1)}, u32[]{:S(2)}) copy-start(bf16[64,128,64]{2,0,1:T(8,128)(2,1)} %get-tuple-element.2) | copy-start | bytes 3145732
  66.5 3.5 %copy-start.2 = (bf16[64,128,64]{2,0,1:T(8,128)(2,1)S(1)}, bf16[64,128,64]{2,0,1:T(8,128)(2,1)}, u32[]{:S(2)}) copy-start(bf16[64,128,64]{2,0,1:T(8,128)(2,1)} %get-tuple-element.3) | copy-start | bytes 3145732
Sparse Core Ops, SparseCore 0:
  10.1 53.0 all-gather.1
  103.6 102.2 reduce-scatter.1
where the time goes:
time: 215 us
  waiting for transfers between devices  86.5 us (40%)
  blocking collectives  61.6 us (29%)
  matrix products  34.5 us (16%)
  other arithmetic  16.6 us (8%)
  between operations  14.2 us (7%)
    psum x1, blocking collectives, shards(): mass = lax.psum(local_mass, 'dp')  61.6 us
    all_gather x1, waiting for transfers between devices, shards(): all_refs = lax.all_gather(refs, 'dp', axis=0, tiled=True)  46.6 us
    reduce_scatter x1, waiting for transfers between devices, shards(): lax.psum_scatter(term - jnp.einsum('mnk,nmq->mkq', post_imag, part_turned...  39.1 us
    dot_general x1, matrix products, shards(): jnp.einsum('mnk,nmq->mkq', post_imag, part_turned, preferred_element_type...  6.76 us
    dot_general x1, matrix products, shards(): corr = jnp.einsum('mnk,mj->jnk', cross_real, part_cos, precision=highest)  5.3 us
    dot_general x1, matrix products, shards(): jnp.einsum('mnk,mj->jnk', cross_imag, part_sin, precision=highest)  4.69 us
  transfers between devices with their start and end apart: 2, of which 2 were waited for; matrix products, arithmetic and copies ran while one was open for 5% of the time, Pallas kernels for 0%

commit v1 on v0

--- a/solution.py
+++ b/solution.py
@@ -32,7 +32,10 @@
     gain = jnp.dot(onehot, gain_table, precision=highest)
     weighted = (particles.astype(jnp.float32) * gain[:, None, :]).astype(jnp.bfloat16)
     turned = jnp.concatenate([weighted[:, :, R:], -weighted[:, :, :R]], axis=2)
-    all_refs = lax.all_gather(refs, "dp", axis=0, tiled=True)
+    count = lax.axis_size("dp")
+    parts = jnp.stack([refs for _ in range(count)])
+    parts = lax.all_to_all(parts, "dp", split_axis=0, concat_axis=0)
+    all_refs = jnp.concatenate(parts, axis=0)
     part_weighted = weighted
     part_turned = turned
     part_cos = cos_table

time: 215 us -> 263 us (1.22)
  waiting for transfers between devices: 86.5 us -> 110 us
  blocking collectives: 61.6 us -> 78.1 us
  starting transfers between devices: 0.08 us -> 7.62 us
  local copies, waits for them, and re-layouts: 1.12 us -> 4.28 us
  other arithmetic: 16.6 us -> 13.5 us
    all_to_all x0 -> x1, waiting for transfers between devices: none -> 71.4 us  [shards(): parts = lax.all_to_all(parts, 'dp', split_axis=0, concat_axis=0)]
    all_gather x1 -> x0, waiting for transfers between devices: 46.6 us -> none  [shards(): all_refs = lax.all_gather(refs, 'dp', axis=0, tiled=True)]
    psum x1, blocking collectives: 61.6 us -> 78.1 us  [shards(): mass = lax.psum(local_mass, 'dp')]
    all_to_all x0 -> x1, starting transfers between devices: none -> 7.58 us  [shards(): parts = lax.all_to_all(parts, 'dp', split_axis=0, concat_axis=0)]
    another operation x0 -> x1, local copies, waits for them, and re-layouts: none -> 3.05 us  [shards(): parts = jnp.stack([refs for _ in range(count)])]
  transfers between devices with their start and end apart: 2 -> 2, of which waited for: 2 -> 2; matrix products, arithmetic and copies ran while one was open for 5% -> 3% of each run, Pallas kernels for 0% -> 0%
where the time goes in v1:
time: 263 us
  waiting for transfers between devices  110 us (42%)
  blocking collectives  78.1 us (30%)
  matrix products  34.8 us (13%)
  between operations  14.2 us (5%)
  other arithmetic  13.5 us (5%)
  starting transfers between devices  7.62 us (3%)
  local copies, waits for them, and re-layouts  4.28 us (2%)
    psum x1, blocking collectives, shards(): mass = lax.psum(local_mass, 'dp')  78.1 us
    all_to_all x1, waiting for transfers between devices, shards(): parts = lax.all_to_all(parts, 'dp', split_axis=0, concat_axis=0)  71.4 us
    reduce_scatter x1, waiting for transfers between devices, shards(): lax.psum_scatter(term - jnp.einsum('mnk,nmq->mkq', post_imag, part_turned...  39.1 us
    all_to_all x1, starting transfers between devices, shards(): parts = lax.all_to_all(parts, 'dp', split_axis=0, concat_axis=0)  7.58 us
    dot_general x1, matrix products, shards(): jnp.einsum('mnk,nmq->mkq', post_imag, part_turned, preferred_element_type...  6.76 us
  transfers between devices with their start and end apart: 2, of which 2 were waited for; matrix products, arithmetic and copies ran while one was open for 3% of the time, Pallas kernels for 0%

profile of v1, /device:TPU:0, one launch (start us, length us, event | category | flops | bytes accessed | tf_op | source)
XLA Modules:
  0.0 263.1 jit_solution(4533943736717276272)
XLA Ops:
  7.2 1.1 copy.11
  8.3 3.0 %stack.2 = bf16[16,8,128,128]{2,3,1,0:T(8,128)(2,1)} broadcast(bf16[8,128,128]{1,2,0:T(8,128)(2,1)S(1)} %copy.11), dimensions={1,2,3} | broadcast | bytes 4456448 | tf_op jit(solution)/shard_map/stack | solution.py:36
  11.3 7.6 %all-to-all-start = ((bf16[16,8,128,128]{2,3,1,0:T(8,128)(2,1)}), bf16[16,8,128,128]{2,3,1,0:T(8,128)(2,1)}, u32[]{:S(2)}, u32[]{:S(2)}) async-start(bf16[16,8,128,128]{2,3,1,0:T(8,128)(2,1)} %stack.2), calls=%async_computation | async-start | bytes 8388608 | tf_op jit(solution)/shard_map/all_to_all | solution.py:37
  19.4 2.9 %multiply_convert_fusion = bf16[64,128,128]{2,0,1:T(8,128)(2,1)S(1)} fusion(bf16[64,128,128]{2,1,0:T(8,128)(2,1)} %param.6, f32[64,128]{1,0:T(8,128)S(1)} %fusion.20), kind=kLoop, calls=%fused_computation.10 | loop fusion | flops 3145728 | bytes 4227072 | tf_op jit(solution)/shard_map/convert_element_type | solution.py:33
  22.4 2.7 %fusion.70 = (bf16[64,128,64]{2,0,1:T(8,128)(2,1)}, bf16[64,128,64]{2,0,1:T(8,128)(2,1)}) fusion(bf16[64,128,128]{2,0,1:T(8,128)(2,1)S(1)} %multiply_convert_fusion), kind=kLoop, calls=%fused_computation.78 | loop fusion | flops 524288 | bytes 4194304 | tf_op jit(solution)/shard_map/slice | solution.py:34
  25.1 71.4 %all-to-all-done = bf16[16,8,128,128]{2,3,1,0:T(8,128)(2,1)} async-done(((bf16[16,8,128,128]{2,3,1,0:T(8,128)(2,1)}), bf16[16,8,128,128]{2,3,1,0:T(8,128)(2,1)}, u32[]{:S(2)}, u32[]{:S(2)}) %all-to-all-start) | async-done | bytes 4194336 | tf_op jit(solution)/shard_map/all_to_all | solution.py:37
  96.5 3.3 %bitcast_convert_fusion = f32[128,128,128]{1,2,0:T(8,128)S(1)} fusion(bf16[16,8,128,128]{2,3,1,0:T(8,128)(2,1)} %all-to-all-done), kind=kLoop, calls=%fused_computation.67 | loop fusion | flops 2097152 | bytes 12582912 | tf_op jit(solution)/shard_map/convert_element_type | solution.py:51
  99.7 0.6 fusion.1
  100.4 0.3 fusion.54
  100.9 3.6 %fusion.72 = f32[128,64,128]{2,1,0:T(8,128)S(1)} fusion(bf16[64,128,128]{2,0,1:T(8,128)(2,1)S(1)} %multiply_convert_fusion, bf16[128,128,128]{1,2,0:T(8,128)(2,1)} %bitcast.1), kind=kOutput, calls=%fused_computation.80 | convolution fusion | flops 268435456 | bytes 10485760 | tf_op jit(solution)/shard_map/nmq,mkq->mnk/dot_general | solution.py:43
  104.5 3.5 %fusion.18 = f32[128,64,128]{2,1,0:T(8,128)S(1)} fusion(bf16[128,128,128]{1,2,0:T(8,128)(2,1)} %bitcast.1, bf16[64,128,64]{2,0,1:T(8,128)(2,1)S(1)} %copy-done.1, bf16[64,128,64]{2,0,1:T(8,128)(2,1)S(1)} %copy-done), kind=kOutput, calls=%fused_computation.23 | convolution fusion | flops 272629760 | bytes 10485760 | tf_op jit(solution)/shard_map/nmq,mkq->mnk/dot_general | solution.py:46
  108.0 4.7 %fusion.2 = f32[36,64,128]{2,0,1:T(8,128)S(1)} fusion(f32[128,64,128]{2,1,0:T(8,128)S(1)} %fusion.18, f32[128]{0:T(128)S(1)} %iota_multiply_fusion), kind=kOutput, calls=%fused_computation.6 | convolution fusion | flops 452994048 | bytes 5374464 | tf_op jit(solution)/shard_map/mnk,mj->jnk/dot_general | solution.py:50
  112.7 5.2 %fusion.71 = (f32[64]{0:T(128)S(1)}, f32[36,64,128]{2,0,1:T(8,128)S(1)}) fusion(f32[128]{0:T(128)S(1)} %log.6, f32[64,128]{1,0:T(8,128)S(1)} %convolution_multiply_fusion, f32[36,64,128]{2,0,1:T(8,128)S(1)} %fusion.2, f32[128,64,128]{2,1,0:T(8,128)S(1)} %fusion.72, f32[128]{0:T(128)S(1)} %iota_multiply_fusion), kind=kOutput, calls=%fused_computation.79 | convolution fusion | flops 454173632 | bytes 6587648 | tf_op jit(solution)/shard_map/mnk,mj->jnk/dot_general | solution.py:49
  117.9 1.0 fusion.17
  118.9 3.9 %fusion.24 = bf16[128,64,128]{2,0,1:T(8,128)(2,1)S(1)} fusion(f32[128]{0:T(128)S(1)} %iota_multiply_fusion, f32[36,64,128]{2,0,1:T(8,128)S(1)} %get-tuple-element.5, f32[64]{0:T(128)S(1)} %fusion.17, f32[64]{0:T(128)S(1)} %get-tuple-element.4), kind=kOutput, calls=%fused_computation.34 | convolution fusion | flops 453583872 | bytes 3277824 | tf_op jit(solution)/shard_map/jnk,mj->mnk/dot_general | solution.py:66
  122.8 3.9 %fusion.21 = bf16[128,64,128]{2,0,1:T(8,128)(2,1)S(1)} fusion(f32[128]{0:T(128)S(1)} %iota_multiply_fusion, f32[36,64,128]{2,0,1:T(8,128)S(1)} %get-tuple-element.5, f32[64]{0:T(128)S(1)} %fusion.17, f32[64]{0:T(128)S(1)} %get-tuple-element.4), kind=kOutput, calls=%fused_computation.31 | convolution fusion | flops 453583872 | bytes 3277824 | tf_op jit(solution)/shard_map/jnk,mj->mnk/dot_general | solution.py:69
  126.7 2.0 fusion.6
  128.7 6.8 %convolution_subtract_fusion = f32[128,128,128]{2,1,0:T(8,128)} fusion(f32[128,128,128]{2,1,0:T(8,128)S(1)} %fusion.6, bf16[128,64,128]{2,0,1:T(8,128)(2,1)S(1)} %fusion.21, bf16[64,128,64]{2,0,1:T(8,128)(2,1)S(1)} %copy-done.1, bf16[64,128,64]{2,0,1:T(8,128)(2,1)S(1)} %copy-done), kind=kOutput, calls=%fused_computation.11 | convolution fusion | flops 274726912 | bytes 20971520 | tf_op jit(solution)/shard_map/mnk,nmq->mkq/dot_general | solution.py:77
  135.4 0.4 fusion.67
  136.1 78.1 %psum.7 = f32[32,128]{1,0:T(8,128)S(1)} all-reduce(f32[32,128]{1,0:T(8,128)S(1)} %fusion.19), channel_id=1, replica_groups=mesh['groups'=2,'dp'=16] {'dp'}, use_global_device_ids=true, to_apply=%region_5.0 | all-reduce | flops 4096 | bytes 32768 | tf_op jit(solution)/shard_map/psum | solution.py:63
  214.2 0.4 convolution_add_fusion
  214.7 0.5 log_add_fusion
  215.3 39.1 %reduce-scatter.2.cloned.1.call-done = f32[8,128,128]{2,1,0:T(8,128)} async-done(((f32[128,128,128]{2,1,0:T(8,128)}), f32[8,128,128]{2,1,0:T(8,128)}) %reduce-scatter.2.cloned.1.call-update) | async-done | bytes 524304 | tf_op jit(solution)/shard_map/reduce_scatter | solution.py:75
  254.3 1.9 broadcast_divide_fusion
  (24 shorter events, 1.0 us)
Async XLA Ops:
  11.3 7.7 %copy-start.3 = (f32[128]{0:T(128)S(1)}, f32[128]{0:T(128)}, u32[]{:S(2)}) copy-start(f32[128]{0:T(128)} %param.10) | copy-start | bytes 1540
  11.3 7.7 %copy-start.4 = (f32[32]{0:T(128)S(1)}, f32[32]{0:T(128)}, u32[]{:S(2)}) copy-start(f32[32]{0:T(128)} %param.9) | copy-start | bytes 388
  11.3 7.7 %copy-start.2 = (f32[64]{0:T(128)S(1)}, f32[64]{0:T(128)}, u32[]{:S(2)}) copy-start(f32[64]{0:T(128)} %param.11) | copy-start | bytes 772
  11.3 7.9 %copy-start.5 = (s32[64]{0:T(128)S(1)}, s32[64]{0:T(128)}, u32[]{:S(2)}) copy-start(s32[64]{0:T(128)} %param.8) | copy-start | bytes 772
  11.3 85.1 %all-to-all-start = ((bf16[16,8,128,128]{2,3,1,0:T(8,128)(2,1)}), bf16[16,8,128,128]{2,3,1,0:T(8,128)(2,1)}, u32[]{:S(2)}, u32[]{:S(2)}) async-start(bf16[16,8,128,128]{2,3,1,0:T(8,128)(2,1)} %stack.2), calls=%async_computation | async-start | bytes 8388608 | tf_op jit(solution)/shard_map/all_to_all | solution.py:37
  18.9 235.4 %reduce-scatter.2.cloned.1.call-start = ((), (), s32[]{:S(2)}) async-start(), calls=%async_computation.2 | async-start | bytes 8912896 | tf_op jit(solution)/shard_map/reduce_scatter | solution.py:75
  100.9 3.6 %copy-start = (bf16[64,128,64]{2,0,1:T(8,128)(2,1)S(1)}, bf16[64,128,64]{2,0,1:T(8,128)(2,1)}, u32[]{:S(2)}) copy-start(bf16[64,128,64]{2,0,1:T(8,128)(2,1)} %get-tuple-element.2) | copy-start | bytes 3145732
  100.9 3.6 %copy-start.1 = (bf16[64,128,64]{2,0,1:T(8,128)(2,1)S(1)}, bf16[64,128,64]{2,0,1:T(8,128)(2,1)}, u32[]{:S(2)}) copy-start(bf16[64,128,64]{2,0,1:T(8,128)(2,1)} %get-tuple-element.3) | copy-start | bytes 3145732
Sparse Core Ops, SparseCore 0:
  135.6 118.7 reduce-scatter.1
